TPU v7x, 32 devices: a whole 2x2x4 slice. The times are simulated.
32 devices in a mesh: slab: 32 (over z, y, x, core).
Axes of the slice: x: 2, y: 2, z: 4, core: 2. Of those that a mesh axis runs over, the one named last changes fastest.
Arguments:
- tensor: float32 [128, 1024, 512], P('slab'), may hold values from 0 to 1024
- first: float32 [128, 512], P('slab'), may hold values from 0.01 to 2.01
- second: float32 [1024, 512], replicated, may hold values from 0.01 to 2.01
- third: float32 [512, 512], replicated, may hold values from 0.01 to 2.01
Outputs:
- new_first: float32 [128, 512], P('slab')
- new_second: float32 [1024, 512], P('slab')
- new_third: float32 [512, 512], P('slab')
All inputs are finite; a program needn't handle non-finite values.
Results may differ from a plain program's by a relative error of at most 0.0002.
Values sent between devices are 32-bit elements; how exact they have to be, the bound alone decides.
No kernel may reach another device: no remote copies, remote signals or barrier semaphores. Data moves between devices by JAX's collectives and lax.ppermute only.
A program may use at most 64 MiB of HBM per device.

v0:
```python
import jax
import jax.numpy as jnp
from jax import lax
from jax.sharding import PartitionSpec as P


def update(start_rows, sums, gram):
    highest = lax.Precision.HIGHEST
    lipschitz = jnp.max(jnp.sum(gram, axis=1))
    previous = start_rows
    extrapolated = start_rows
    updated = start_rows
    for turn in range(4):
        gradient = jnp.dot(extrapolated, gram, precision=highest) - sums
        updated = jnp.maximum(extrapolated - gradient / lipschitz, 0.0)
        extrapolated = updated + turn / (turn + 3.0) * (updated - previous)
        previous = updated
    return updated


def body(tensor, first, second, third):
    highest = lax.Precision.HIGHEST
    devices_count = lax.axis_size("slab")
    device_index = lax.axis_index("slab")
    second_count = second.shape[0] // devices_count
    third_count = third.shape[0] // devices_count
    gram_second = jnp.dot(second.T, second, precision=highest)
    gram_third = jnp.dot(third.T, third, precision=highest)
    partial_value = jnp.einsum("ijk,kr->ijr", tensor, third, precision=highest)
    first_sums = jnp.einsum("ijr,jr->ir", partial_value, second, precision=highest)
    new_first = update(first, first_sums, gram_second * gram_third)
    own_gram = jnp.dot(new_first.T, new_first, precision=highest)
    gram_first = lax.psum(own_gram, "slab")
    own_term = jnp.einsum("ijr,ir->jr", partial_value, new_first, precision=highest)
    second_sums = lax.psum(own_term, "slab")
    whole_second = update(second, second_sums, gram_first * gram_third)
    weighted = whole_second[None, :, :] * new_first[:, None, :]
    third_sums = jnp.einsum("ijk,ijr->kr", tensor, weighted, precision=highest)
    gram_new_second = jnp.dot(whole_second.T, whole_second, precision=highest)
    out_second = lax.dynamic_slice_in_dim(
        whole_second, device_index * second_count, second_count, 0
    )
    third_rows = lax.psum_scatter(third_sums, "slab", scatter_dimension=0, tiled=True)
    own_third = lax.dynamic_slice_in_dim(third, device_index * third_count, third_count, 0)
    new_third = update(own_third, third_rows, gram_first * gram_new_second)
    return (new_first, out_second, new_third)


def solution(mesh):
    in_specs = (P("slab", None, None), P("slab", None), P(), P())
    out_specs = (P("slab", None), P("slab", None), P("slab", None))
    return jax.shard_map(body, mesh=mesh, in_specs=in_specs, out_specs=out_specs, check_vma=False)
```

profile of v0, /device:TPU:0, one launch (start us, length us, event | category | flops | bytes accessed | tf_op | source)
XLA Modules:
  0.0 380.0 jit_solution(14814584285607130259)
XLA Ops:
  7.2 0.0 copy-start
  7.2 0.0 all-reduce.3.cloned.1.call-start
  7.2 3.5 fusion.82
  10.8 0.0 copy-done
  10.8 0.0 copy-start.1
  10.8 3.6 fusion.80
  14.4 0.0 copy-done.1
  14.4 0.6 reduce_max.27
  15.0 0.0 copy-start.7
  15.0 16.6 %multiply_reduce_fusion.1 = (f32[512,4]{0,1:T(4,128)S(1)}, f32[4,1024,512]{2,1,0:T(8,128)S(1)}) fusion(f32[512,1024]{0,1:T(8,128)S(1)} %bitcast.64, f32[4,1024,512]{2,1,0:T(8,128)} %param.4, f32[512,512]{1,0:T(8,128)} %param.7), kind=kOutput, calls=%fused_computation.1 | convolution fusion | flops 12889094144 | bytes 19931136 | tf_op jit(solution)/shard_map/ijk,kr->ijr/dot_general | solution.py:29
  31.6 0.0 copy-done.7
  31.7 1.6 fusion.35
  33.3 1.6 fusion.31
  34.9 1.6 fusion.28
  36.5 1.6 fusion.25
  38.2 0.0 copy-start.6
  38.2 2.1 fusion.83
  40.3 2.5 multiply_reduce_fusion
  42.8 2.9 copy.28
  45.7 0.0 all-reduce.3.cloned.1.call-update
  45.7 0.0 copy-start.2
  45.7 0.0 reduce-scatter.2.cloned.1.call-start
  45.8 1.9 copy.8
  47.6 139.1 %all-reduce.3.cloned.1.call-done = (f32[1024,512]{0,1:T(8,128)}, f32[512,512]{0,1:T(8,128)}) async-done(((f32[1024,512]{0,1:T(8,128)}, f32[512,512]{0,1:T(8,128)}), (f32[1024,512]{0,1:T(8,128)}, f32[512,512]{0,1:T(8,128)})) %all-reduce.3.cloned.1.call-update) | async-done | bytes 3145744 | tf_op jit(solution)/shard_map/psum | solution.py:35
  186.7 0.0 copy-done.2
  186.7 2.4 fusion.79
  189.1 0.6 reduce_max.28
  189.7 0.0 copy-start.3
  189.7 0.0 copy-start.4
  189.7 8.0 %fusion.6 = f32[1024,512]{0,1:T(8,128)S(1)} fusion(f32[1024,512]{0,1:T(8,128)} %copy.8, f32[1024,512]{0,1:T(8,128)} %get-tuple-element.6, f32[512,512]{0,1:T(8,128)} %get-tuple-element.9, f32[1024,512]{1,0:T(8,128)S(1)} %copy-done, f32[]{:T(128)} %reduce_max.28), kind=kOutput, calls=%fused_computation.9 | convolution fusion | flops 3223322624 | bytes 9437188 | tf_op jit(solution)/shard_map/dot_general | solution.py:14
  197.7 0.0 copy-done.3
  197.7 0.0 copy-done.4
  197.7 0.0 copy-start.8
  197.7 0.0 slice-start
  197.7 3.7 fusion.40
  201.5 0.0 copy-done.8
  201.5 0.0 slice-start.1
  201.5 6.0 %multiply_add_fusion = f32[1024,512]{0,1:T(8,128)S(1)} fusion(f32[1024,512]{0,1:T(8,128)S(1)} %copy-done.8, f32[1024,512]{0,1:T(8,128)S(1)} %fusion.6, f32[512,512]{0,1:T(8,128)S(1)} %copy-done.4, f32[1024,512]{0,1:T(8,128)S(1)} %fusion.40, f32[1024,512]{0,1:T(8,128)S(1)} %copy-done.3, f32[]{:T(128)} %reduce_max.28), kind=kOutput, calls=%fused_computation.11 | convolution fusion | flops 3235381248 | bytes 11534340 | tf_op jit(solution)/shard_map/dot_general | solution.py:14
  207.5 4.6 %subtract_maximum_fusion = f32[1024,512]{0,1:T(8,128)S(1)} fusion(f32[1024,512]{0,1:T(8,128)S(1)} %multiply_add_fusion, f32[1024,512]{0,1:T(8,128)S(1)} %copy-done.8, f32[512,512]{0,1:T(8,128)S(1)} %copy-done.4, f32[]{:T(128)} %reduce_max.28), kind=kOutput, calls=%fused_computation.10 | convolution fusion | flops 3223322624 | bytes 7340036 | tf_op jit(solution)/shard_map/dot_general | solution.py:14
  212.1 0.0 copy-done.6
  212.2 0.0 slice-done
  212.2 0.0 slice-done.1
  212.2 16.2 %fusion.8 = f32[512,512]{1,0:T(8,128)} fusion(f32[4,1024,512]{2,1,0:T(8,128)S(1)} %bitcast.66, f32[4,512]{1,0:T(4,128)S(1)} %fusion.25, f32[1024,512]{0,1:T(8,128)S(1)} %subtract_maximum_fusion), kind=kOutput, calls=%fused_computation.16 | convolution fusion | flops 12886999040 | bytes 11542528 | tf_op jit(solution)/shard_map/ijk,ijr->kr/dot_general | solution.py:38
  228.3 0.0 reduce-scatter.2.cloned.1.call-update
  228.4 4.7 %fusion.81 = (f32[512]{0:T(512)S(1)}, f32[512,512]{0,1:T(8,128)S(1)}) fusion(f32[512,512]{0,1:T(8,128)} %get-tuple-element.7, f32[1024,512]{0,1:T(8,128)S(1)} %subtract_maximum_fusion), kind=kOutput, calls=%fused_computation.98 | convolution fusion | flops 3221749248 | bytes 4196352 | tf_op jit(solution)/shard_map/dot_general | solution.py:39
  233.1 0.6 reduce_max.29
  233.7 0.1 constant_dynamic-slice_fusion
  233.9 0.7 copy.14
  234.6 129.6 %reduce-scatter.2.cloned.1.call-done = f32[16,512]{1,0:T(8,128)} async-done(((f32[512,512]{1,0:T(8,128)}), f32[16,512]{1,0:T(8,128)}) %reduce-scatter.2.cloned.1.call-update) | async-done | bytes 32784 | tf_op jit(solution)/shard_map/reduce_scatter | solution.py:43
  364.2 0.0 copy-start.5
  364.2 2.5 fusion.22
  366.6 2.4 fusion.19
  369.1 0.0 copy-done.5
  369.1 1.6 fusion.16
  370.7 2.2 fusion.13
  (1 shorter events, 0.0 us)
Async XLA Ops:
  7.2 3.6 copy-start
  7.2 179.5 %all-reduce.3.cloned.1.call-start = ((), (), s32[]{:S(2)}) async-start(), calls=%async_computation.2 | async-start | bytes 6291456 | tf_op jit(solution)/shard_map/psum | solution.py:35
  10.8 3.6 copy-start.1
  15.0 16.6 %copy-start.7 = (f32[4,512]{1,0:T(4,128)S(1)}, f32[4,512]{1,0:T(4,128)}, u32[]{:S(2)}) copy-start(f32[4,512]{1,0:T(4,128)} %param.5) | copy-start | bytes 24580
  38.2 174.0 %copy-start.6 = (f32[4,512]{1,0:T(4,128)}, f32[4,512]{1,0:T(4,128)S(1)}, u32[]{:S(2)}) copy-start(f32[4,512]{1,0:T(4,128)S(1)} %fusion.25) | copy-start | bytes 24580
  45.7 141.0 %copy-start.2 = (f32[512,512]{0,1:T(8,128)S(1)}, f32[512,512]{0,1:T(8,128)}, u32[]{:S(2)}) copy-start(f32[512,512]{0,1:T(8,128)} %copy-done.1) | copy-start | bytes 3145732
  45.7 318.5 %reduce-scatter.2.cloned.1.call-start = ((), (), s32[]{:S(2)}) async-start(), calls=%async_computation.1 | async-start | bytes 1081344 | tf_op jit(solution)/shard_map/reduce_scatter | solution.py:43
  189.7 8.0 %copy-start.3 = (f32[1024,512]{0,1:T(8,128)S(1)}, f32[1024,512]{0,1:T(8,128)}, u32[]{:S(2)}) copy-start(f32[1024,512]{0,1:T(8,128)} %copy.8) | copy-start | bytes 6291460
  189.7 8.0 %copy-start.4 = (f32[512,512]{0,1:T(8,128)S(1)}, f32[512,512]{0,1:T(8,128)}, u32[]{:S(2)}) copy-start(f32[512,512]{0,1:T(8,128)} %get-tuple-element.9) | copy-start | bytes 3145732
  197.7 3.8 copy-start.8
  197.7 14.4 %slice-start = ((s8[8388608]{0:T(1024)(128)(4,1)}), s8[4194304]{0:T(1024)(128)(4,1)S(1)}, s32[]{:S(2)}) async-start(s8[8388608]{0:T(1024)(128)(4,1)} %bitcast.65), calls=%async_computation.3 | async-start | bytes 8388608
  201.5 10.7 %slice-start.1 = ((s8[8388608]{0:T(1024)(128)(4,1)}), s8[4194304]{0:T(1024)(128)(4,1)S(1)}, s32[]{:S(2)}) async-start(s8[8388608]{0:T(1024)(128)(4,1)} %bitcast.65), calls=%async_computation.4 | async-start | bytes 8388608
  364.2 4.9 %copy-start.5 = (f32[16,512]{1,0:T(8,128)S(1)}, f32[16,512]{1,0:T(8,128)}, u32[]{:S(2)}) copy-start(f32[16,512]{1,0:T(8,128)} %reduce-scatter.2.cloned.1.call-done) | copy-start | bytes 98308
Sparse Core Ops, SparseCore 0:
  45.8 140.8 all-reduce.2
  228.5 135.6 reduce-scatter.1
where the time goes:
time: 385 us; the launch traced here: 380 us
  waiting for transfers between devices  269 us (70%)
  matrix products  84.4 us (22%)
  between operations  14.5 us (4%)
  other arithmetic  6.73 us (2%)
  local copies, waits for them, and re-layouts  5.68 us (1%)
    psum x1, waiting for transfers between devices, body(): second_sums = lax.psum(own_term, 'slab')  139 us
    reduce_scatter x1, waiting for transfers between devices, body(): lax.psum_scatter(third_sums, 'slab', scatter_dimension=0, tiled=True)  130 us
    dot_general x12, matrix products, update(): gradient = jnp.dot(extrapolated, gram, precision=highest) - sums  37.6 us
    dot_general x1, matrix products, body(): partial_value = jnp.einsum('ijk,kr->ijr', tensor, third, precision=highest)  16.6 us
    dot_general x1, matrix products, body(): third_sums = jnp.einsum('ijk,ijr->kr', tensor, weighted, precision=highest)  16.2 us
  transfers between devices with their start and end apart: 2, of which 2 were waited for; matrix products, arithmetic and copies ran while one was open for 2% of the time, Pallas kernels for 0%

commit v1 on v0

v1 whole, which is shorter than its diff:
```python
import jax
import jax.numpy as jnp
from jax import lax
from jax.sharding import PartitionSpec as P

AXIS = "slab"
PREC = lax.Precision.HIGH


def update(start_rows, sums, gram):
    inverse = 1.0 / jnp.max(jnp.sum(gram, axis=1))
    previous = start_rows
    extrapolated = start_rows
    updated = start_rows
    for turn in range(4):
        gradient = jnp.dot(extrapolated, gram, precision=PREC) - sums
        updated = jnp.maximum(extrapolated - gradient * inverse, 0.0)
        extrapolated = updated + turn / (turn + 3.0) * (updated - previous)
        previous = updated
    return updated


def swap(value, devices_count, mask):
    return lax.ppermute(value, AXIS, [(i, i ^ mask) for i in range(devices_count)])


def pick(value, axis, index):
    return lax.dynamic_index_in_dim(value, index, axis, keepdims=False)


def my_bits(index, bits):
    number = 0
    for place, bit in enumerate(bits):
        number = number + (((index >> bit) & 1) << place)
    return number


def groups_of(bits_count):
    rest = list(range(min(3, bits_count), bits_count))
    return [tuple(rest[i : i + 2]) for i in range(0, len(rest), 2)]


def spread(number, bits):
    return sum(((number >> place) & 1) << bit for place, bit in enumerate(bits))


def scatter_bit(blocks, bits, bit, index, devices_count):
    place = bits.index(bit)
    shape = blocks.shape
    split = blocks.reshape(shape[0] >> (place + 1), 2, 1 << place, *shape[1:])
    mine = (index >> bit) & 1
    away = pick(split, 1, 1 - mine)
    kept = pick(split, 1, mine)
    came = swap(away, devices_count, 1 << bit)
    total = (kept + came).reshape(shape[0] // 2, *shape[1:])
    return total, [b for b in bits if b != bit]


def reduce_scatter(blocks, index, devices_count):
    bits = list(range(devices_count.bit_length() - 1))
    all_bits = len(bits)
    if 0 in bits:
        blocks, bits = scatter_bit(blocks, bits, 0, index, devices_count)
    half = blocks.shape[-1] // 2
    lanes = [blocks[..., :half], blocks[..., half:]]
    orders = [[b for b in (1, 2) if b in bits], [b for b in (2, 1) if b in bits]]
    left = bits
    for lane in range(2):
        left = bits
        for bit in orders[lane]:
            lanes[lane], left = scatter_bit(lanes[lane], left, bit, index, devices_count)
    blocks = jnp.concatenate(lanes, axis=-1)
    bits = left
    for group in groups_of(all_bits):
        size = 1 << len(group)
        split = blocks.reshape(blocks.shape[0] // size, size, *blocks.shape[1:])
        mine = my_bits(index, group)
        total = pick(split, 1, mine)
        for turn in range(1, size):
            away = pick(split, 1, mine ^ turn)
            total = total + swap(away, devices_count, spread(turn, group))
        blocks = total
        bits = [b for b in bits if b not in group]
    return blocks[0]


def gather_bits(blocks, bits, group, index, devices_count):
    size = 1 << len(group)
    pieces = [blocks] + [
        swap(blocks, devices_count, spread(turn, group)) for turn in range(1, size)
    ]
    mine = my_bits(index, group)
    stacked = jnp.stack(pieces)
    order = jnp.stack([pick(stacked, 0, mine ^ place) for place in range(size)], axis=1)
    return order.reshape(blocks.shape[0] * size, *blocks.shape[1:]), list(group) + bits


def all_gather(block, index, devices_count):
    bits_count = devices_count.bit_length() - 1
    blocks = block[None]
    bits = []
    for group in reversed(groups_of(bits_count)):
        blocks, bits = gather_bits(blocks, bits, group, index, devices_count)
    half = blocks.shape[-1] // 2
    lanes = [blocks[..., :half], blocks[..., half:]]
    low = [b for b in (2, 1) if b < bits_count]
    for lane in range(2):
        order = low if lane == 0 else low[::-1]
        for bit in order:
            lanes[lane], _ = gather_bits(lanes[lane], [], (bit,), index, devices_count)
    if len(low) == 2:
        shape = lanes[1].shape
        lanes[1] = (
            lanes[1].reshape(shape[0] // 4, 2, 2, *shape[1:]).swapaxes(1, 2).reshape(shape)
        )
    blocks = jnp.concatenate(lanes, axis=-1)
    if bits_count:
        blocks, bits = gather_bits(blocks, [], (0,), index, devices_count)
    return blocks.reshape(-1, block.shape[-1])


def gather_rows(rows, devices_count):
    bits_count = devices_count.bit_length() - 1
    for group in groups_of(bits_count)[::-1] + [(b,) for b in (2, 1, 0) if b < bits_count]:
        pieces = [rows] + [
            swap(rows, devices_count, spread(turn, group)) for turn in range(1, 1 << len(group))
        ]
        rows = jnp.concatenate(pieces, axis=0)
    return rows


def body(tensor, first, second, third):
    devices_count = lax.axis_size(AXIS)
    index = lax.axis_index(AXIS)
    slabs = tensor.shape[0]
    rank = third.shape[1]
    second_count = second.shape[0] // devices_count
    third_count = third.shape[0] // devices_count
    gram_second = jnp.dot(second.T, second, precision=PREC)
    gram_third = jnp.dot(third.T, third, precision=PREC)
    partial_value = jnp.einsum("ijk,kr->ijr", tensor, third, precision=PREC)
    first_sums = jnp.sum(partial_value * second[None], axis=1)
    new_first = update(first, first_sums, gram_second * gram_third)
    every_first = gather_rows(new_first, devices_count)
    gram_first = jnp.dot(every_first.T, every_first, precision=PREC)
    own_term = jnp.sum(partial_value * new_first[:, None, :], axis=0)
    second_rows = reduce_scatter(
        own_term.reshape(devices_count, second_count, rank), index, devices_count
    )
    own_second = lax.dynamic_slice_in_dim(second, index * second_count, second_count, 0)
    out_second = update(own_second, second_rows, gram_first * gram_third)
    whole_second = all_gather(out_second, index, devices_count)
    third_sums = 0.0
    for slab in range(slabs):
        product = lax.dot_general(
            tensor[slab], whole_second, (((0,), (0,)), ((), ())), precision=PREC
        )
        third_sums = third_sums + product * new_first[slab][None, :]
    gram_new_second = jnp.dot(whole_second.T, whole_second, precision=PREC)
    third_rows = reduce_scatter(
        third_sums.reshape(devices_count, third_count, rank), index, devices_count
    )
    own_third = lax.dynamic_slice_in_dim(third, index * third_count, third_count, 0)
    new_third = update(own_third, third_rows, gram_first * gram_new_second)
    return (new_first, out_second, new_third)


def solution(mesh):
    in_specs = (P(AXIS, None, None), P(AXIS, None), P(), P())
    out_specs = (P(AXIS, None), P(AXIS, None), P(AXIS, None))
    return jax.shard_map(body, mesh=mesh, in_specs=in_specs, out_specs=out_specs, check_vma=False)
```

time: 385 us -> 144 us (0.37); the launches traced: 380 us -> 143 us
  waiting for transfers between devices: 269 us -> 40.5 us
  matrix products: 84.4 us -> 40.8 us
  starting transfers between devices: 0.08 us -> 38.7 us
  between operations: 14.5 us -> 3.35 us
  other arithmetic: 6.73 us -> 15.3 us
    psum x1 -> x0, waiting for transfers between devices: 139 us -> none  [body(): second_sums = lax.psum(own_term, 'slab')]
    reduce_scatter x1 -> x0, waiting for transfers between devices: 130 us -> none  [body(): lax.psum_scatter(third_sums, 'slab', scatter_dimension=0, tiled=True)]
    dot_general x18 -> x21, matrix products: 84.4 us -> 40.8 us  [the longest x1 11.6 us: body(): partial_value = jnp.einsum('ijk,kr->ijr', tensor, third, precision=PREC)]
    ppermute x0 -> x30, waiting for transfers between devices: none -> 40.5 us  [swap(): lax.ppermute(value, AXIS, [(i, i ^ mask) for i in range(devices_count)])]
    ppermute x0 -> x30, starting transfers between devices: none -> 38.7 us  [swap(): lax.ppermute(value, AXIS, [(i, i ^ mask) for i in range(devices_count)])]
  transfers between devices with their start and end apart: 2 -> 30, of which waited for: 2 -> 20; matrix products, arithmetic and copies ran while one was open for 2% -> 8% of each run, Pallas kernels for 0% -> 0%
where the time goes in v1:
time: 144 us; the launch traced here: 143 us
  matrix products  40.8 us (28%)
  waiting for transfers between devices  40.5 us (28%)
  starting transfers between devices  38.7 us (27%)
  other arithmetic  15.3 us (11%)
  local copies, waits for them, and re-layouts  4.63 us (3%)
  between operations  3.35 us (2%)
    ppermute x30, waiting for transfers between devices, swap(): lax.ppermute(value, AXIS, [(i, i ^ mask) for i in range(devices_count)])  40.5 us
    ppermute x30, starting transfers between devices, swap(): lax.ppermute(value, AXIS, [(i, i ^ mask) for i in range(devices_count)])  38.7 us
    dot_general x1, matrix products, body(): partial_value = jnp.einsum('ijk,kr->ijr', tensor, third, precision=PREC)  11.6 us
    dot_general x4, matrix products, body(): lax.dot_general(tensor[slab], whole_second, (((0,), (0,)), ((), ())), pre...  11 us
    dot_general x12, matrix products, update(): gradient = jnp.dot(extrapolated, gram, precision=PREC) - sums  8.87 us
    reduce_sum x1, other arithmetic, body(): own_term = jnp.sum(partial_value * new_first[:, None, :], axis=0)  6.15 us
    dot_general x1, matrix products, body(): gram_new_second = jnp.dot(whole_second.T, whole_second, precision=PREC)  3.07 us
  transfers between devices with their start and end apart: 30, of which 20 were waited for; matrix products, arithmetic and copies ran while one was open for 8% of the time, Pallas kernels for 0%

profile of v1, /device:TPU:0, one launch (start us, length us, event | category | flops | bytes accessed | tf_op | source)
XLA Modules:
  0.0 143.3 jit_solution(4904249022553971390)
XLA Ops:
  0.7 2.7 %fusion.172 = f32[512,512]{0,1:T(8,128)S(1)} fusion(f32[512,512]{1,0:T(8,128)} %param.7), kind=kOutput, calls=%fused_computation.249 | convolution fusion | flops 805306368 | bytes 2097152 | tf_op jit(solution)/shard_map/dot_general | solution.py:140
  3.4 11.6 %multiply_reduce_fusion.1 = (f32[4,512]{1,0:T(4,128)S(1)}, f32[4,1024,512]{2,1,0:T(8,128)}) fusion(f32[1024,512]{1,0:T(8,128)S(1)} %copy-done, f32[4,1024,512]{2,1,0:T(8,128)} %param.4, f32[512,512]{1,0:T(8,128)S(1)} %copy-done.1), kind=kOutput, calls=%fused_computation.1 | convolution fusion | flops 6446643200 | bytes 19931136 | tf_op jit(solution)/shard_map/ijk,kr->ijr/dot_general | solution.py:141
  15.0 1.9 %fusion.170 = (f32[512]{0:T(512)S(1)}, f32[512,512]{0,1:T(8,128)S(1)}) fusion(f32[512,512]{0,1:T(8,128)S(1)} %fusion.172, f32[1024,512]{1,0:T(8,128)S(1)} %copy-done), kind=kOutput, calls=%fused_computation.247 | convolution fusion | flops 1611136512 | bytes 4196352 | tf_op jit(solution)/shard_map/dot_general | solution.py:139
  16.9 0.6 reduce_max.27
  20.4 6.1 %multiply_reduce_fusion = f32[1024,512]{1,0:T(8,128)} fusion(f32[4,1024,512]{2,1,0:T(8,128)} %get-tuple-element.44, f32[4,512]{1,0:T(4,128)S(1)} %fusion.60), kind=kLoop, calls=%fused_computation | loop fusion | flops 3670016 | bytes 10493952 | tf_op jit(solution)/shard_map/reduce_sum | solution.py:146
  26.5 1.3 dynamic-slice_bitcast_fusion
  28.4 2.6 %collective-permute-start = (f32[4,512]{1,0:T(4,128)S(1)}, f32[4,512]{1,0:T(4,128)S(1)}, u32[]{:S(2)}, u32[]{:S(2)}) collective-permute-start(f32[4,512]{1,0:T(4,128)S(1)} %fusion.60), channel_id=1, source_target_pairs={{0,8},{1,9},{2,10},{3,11},{4,12},{5,13},{6,14},{7,15},{8,0},{9,1},... | collective-permute-start | bytes 24584 | tf_op jit(solution)/shard_map/ppermute | solution.py:24
  31.1 2.6 %collective-permute-start.1 = (f32[4,512]{1,0:T(4,128)S(1)}, f32[4,512]{1,0:T(4,128)S(1)}, u32[]{:S(2)}, u32[]{:S(2)}) collective-permute-start(f32[4,512]{1,0:T(4,128)S(1)} %fusion.60), channel_id=1, source_target_pairs={{0,16},{1,17},{2,18},{3,19},{4,20},{5,21},{6,22},{7,23},{8,24},{9,... | collective-permute-start | bytes 24584 | tf_op jit(solution)/shard_map/ppermute | solution.py:24
  33.7 2.0 %collective-permute-done.1 = f32[4,512]{1,0:T(4,128)S(1)} collective-permute-done((f32[4,512]{1,0:T(4,128)S(1)}, f32[4,512]{1,0:T(4,128)S(1)}, u32[]{:S(2)}, u32[]{:S(2)}) %collective-permute-start.1) | collective-permute-done | bytes 8224 | tf_op jit(solution)/shard_map/ppermute | solution.py:24
  35.6 3.5 %collective-permute-done.2 = f32[4,512]{1,0:T(4,128)S(1)} collective-permute-done((f32[4,512]{1,0:T(4,128)S(1)}, f32[4,512]{1,0:T(4,128)S(1)}, u32[]{:S(2)}, u32[]{:S(2)}) %collective-permute-start.2) | collective-permute-done | bytes 8224 | tf_op jit(solution)/shard_map/ppermute | solution.py:24
  39.1 1.6 %collective-permute-start.3 = (f32[16,512]{1,0:T(8,128)S(1)}, f32[16,512]{1,0:T(8,128)S(1)}, u32[]{:S(2)}, u32[]{:S(2)}) collective-permute-start(f32[16,512]{1,0:T(8,128)S(1)} %pad_maximum_fusion.7), channel_id=1, source_target_pairs={{0,4},{1,5},{2,6},{3,7},{4,0},{5,1},{6,2},{7,3},{8,12},{9,13},{10,... | collective-permute-start | bytes 98312 | tf_op jit(solution)/shard_map/ppermute | solution.py:24
  40.7 2.4 %collective-permute-done.3 = f32[16,512]{1,0:T(8,128)S(1)} collective-permute-done((f32[16,512]{1,0:T(8,128)S(1)}, f32[16,512]{1,0:T(8,128)S(1)}, u32[]{:S(2)}, u32[]{:S(2)}) %collective-permute-start.3) | collective-permute-done | bytes 32800 | tf_op jit(solution)/shard_map/ppermute | solution.py:24
  43.2 1.6 %collective-permute-start.4 = (f32[32,512]{1,0:T(8,128)S(1)}, f32[32,512]{1,0:T(8,128)S(1)}, u32[]{:S(2)}, u32[]{:S(2)}) collective-permute-start(f32[32,512]{1,0:T(8,128)S(1)} %concatenate.26), channel_id=1, source_target_pairs={{0,2},{1,3},{2,0},{3,1},{4,6},{5,7},{6,4},{7,5},{8,10},{9,11},{10,... | collective-permute-start | bytes 196616 | tf_op jit(solution)/shard_map/ppermute | solution.py:24
  44.7 1.8 %fusion.75 = f32[16,32,512]{2,1,0:T(8,128)S(1)} fusion(f32[16,1,32,512]{3,2,0,1:T(8,128)} %collective-permute-done.6, f32[16,2,1,32,512]{4,3,1,0,2:T(8,128)} %bitcast.203, s32[]{:T(128)S(6)} %select_n.95), kind=kLoop, calls=%fused_computation.84 | loop fusion | flops 262144 | bytes 3145732 | tf_op jit(solution)/shard_map/reshape | solution.py:55
  46.6 0.7 dynamic-slice_bitcast_fusion.2
  48.1 1.4 collective-permute-done.5
  49.5 1.0 concatenate.28
  50.5 1.6 %collective-permute-start.9 = (f32[4,2,32,256]{3,2,0,1:T(8,128)S(1)}, f32[4,2,32,256]{3,2,0,1:T(8,128)S(1)}, u32[]{:S(2)}, u32[]{:S(2)}) collective-permute-start(f32[4,2,32,256]{3,2,0,1:T(8,128)S(1)} %bitcast.227), channel_id=1, source_target_pairs={{0,4},{1,5},{2,6},{3,7},{4,0},{5,1},{6,2},{7,3},{8,12},{9,13},{10,... | collective-permute-start | bytes 786440 | tf_op jit(solution)/shard_map/ppermute | solution.py:24
  52.1 1.9 %collective-permute-done.7 = f32[8,1,32,256]{3,2,0,1:T(8,128)} collective-permute-done((f32[8,1,32,256]{3,2,0,1:T(8,128)}, f32[8,1,32,256]{3,2,0,1:T(8,128)}, u32[]{:S(2)}, u32[]{:S(2)}) %collective-permute-start.7) | collective-permute-done | bytes 262176 | tf_op jit(solution)/shard_map/ppermute | solution.py:24
  54.1 1.0 bitcast_add_fusion.2
  55.1 1.6 %collective-permute-start.8 = (f32[4,1,32,256]{3,2,0,1:T(8,128)S(1)}, f32[4,1,32,256]{3,2,0,1:T(8,128)S(1)}, u32[]{:S(2)}, u32[]{:S(2)}) collective-permute-start(f32[4,1,32,256]{3,2,0,1:T(8,128)S(1)} %dynamic-slice_bitcast_fusion.4), channel_id=1, source_target_pairs={{0,4},{1,5},{2,6},{3,7},{4,0},{5,1},{6,2},{7,3},{8,12},{9,13},{10,... | collective-permute-start | bytes 393224 | tf_op jit(solution)/shard_map/ppermute | solution.py:24
  56.7 3.1 %collective-permute-done.9 = f32[4,2,32,256]{3,2,0,1:T(8,128)S(1)} collective-permute-done((f32[4,2,32,256]{3,2,0,1:T(8,128)S(1)}, f32[4,2,32,256]{3,2,0,1:T(8,128)S(1)}, u32[]{:S(2)}, u32[]{:S(2)}) %collective-permute-start.9) | collective-permute-done | bytes 262176 | tf_op jit(solution)/shard_map/ppermute | solution.py:24
  59.9 1.8 %collective-permute-start.10 = (f32[4,1,32,256]{3,2,0,1:T(8,128)S(1)}, f32[4,1,32,256]{3,2,0,1:T(8,128)S(1)}, u32[]{:S(2)}, u32[]{:S(2)}) collective-permute-start(f32[4,1,32,256]{3,2,0,1:T(8,128)S(1)} %constant_dynamic-slice_fusion.7), channel_id=1, source_target_pairs={{0,2},{1,3},{2,0},{3,1},{4,6},{5,7},{6,4},{7,5},{8,10},{9,11},{10,... | collective-permute-start | bytes 393224 | tf_op jit(solution)/shard_map/ppermute | solution.py:24
  61.8 3.1 %collective-permute-done.10 = f32[4,1,32,256]{3,2,0,1:T(8,128)S(1)} collective-permute-done((f32[4,1,32,256]{3,2,0,1:T(8,128)S(1)}, f32[4,1,32,256]{3,2,0,1:T(8,128)S(1)}, u32[]{:S(2)}, u32[]{:S(2)}) %collective-permute-start.10) | collective-permute-done | bytes 131104 | tf_op jit(solution)/shard_map/ppermute | solution.py:24
  64.9 0.7 fusion.100
  65.7 4.3 %collective-permute-start.11 = (f32[1,32,512]{2,1,0:T(8,128)}, f32[1,32,512]{2,1,0:T(8,128)}, u32[]{:S(2)}, u32[]{:S(2)}) collective-permute-start(f32[1,32,512]{2,1,0:T(8,128)} %get-tuple-element.33), channel_id=1, source_target_pairs={{0,8},{1,9},{2,10},{3,11},{4,12},{5,13},{6,14},{7,15},{8,0},{9,1},... | collective-permute-start | bytes 196616 | tf_op jit(solution)/shard_map/ppermute | solution.py:24
  70.0 1.6 %fusion.165 = (f32[512]{0:T(512)S(1)}, f32[512,512]{0,1:T(8,128)S(1)}, f32[512,512]{0,1:T(8,128)}) fusion(f32[512,512]{0,1:T(8,128)S(1)} %copy-done.3, f32[128,512]{1,0:T(8,128)S(1)} %concatenate.28), kind=kOutput, calls=%fused_computation.242 | convolution fusion | flops 201850368 | bytes 3409920 | tf_op jit(solution)/shard_map/dot_general | solution.py:145
  71.6 0.6 reduce_max.28
  72.9 0.9 fusion.99
  76.2 2.0 %collective-permute-start.16 = (f32[1,32,512]{2,1,0:T(8,128)S(1)}, f32[1,32,512]{2,1,0:T(8,128)S(1)}, u32[]{:S(2)}, u32[]{:S(2)}) collective-permute-start(f32[1,32,512]{2,1,0:T(8,128)S(1)} %bitcast.228), channel_id=1, source_target_pairs={{0,24},{1,25},{2,26},{3,27},{4,28},{5,29},{6,30},{7,31},{8,16},{9,... | collective-permute-start | bytes 196616 | tf_op jit(solution)/shard_map/ppermute | solution.py:24
  78.3 1.1 collective-permute-start.15
  79.4 1.3 collective-permute-start.14
  80.7 1.7 %collective-permute-done.16 = f32[1,32,512]{2,1,0:T(8,128)S(1)} collective-permute-done((f32[1,32,512]{2,1,0:T(8,128)S(1)}, f32[1,32,512]{2,1,0:T(8,128)S(1)}, u32[]{:S(2)}, u32[]{:S(2)}) %collective-permute-start.16) | collective-permute-done | bytes 65568 | tf_op jit(solution)/shard_map/ppermute | solution.py:24
  82.4 1.5 %collective-permute-done.15 = f32[1,32,512]{2,1,0:T(8,128)S(1)} collective-permute-done((f32[1,32,512]{2,1,0:T(8,128)S(1)}, f32[1,32,512]{2,1,0:T(8,128)S(1)}, u32[]{:S(2)}, u32[]{:S(2)}) %collective-permute-start.15) | collective-permute-done | bytes 65568 | tf_op jit(solution)/shard_map/ppermute | solution.py:24
  84.5 1.8 %collective-permute-start.19 = (f32[4,32,256]{2,1,0:T(8,128)S(1)}, f32[4,32,256]{2,1,0:T(8,128)S(1)}, u32[]{:S(2)}, u32[]{:S(2)}) collective-permute-start(f32[4,32,256]{2,1,0:T(8,128)S(1)} %get-tuple-element.26), channel_id=1, source_target_pairs={{0,2},{1,3},{2,0},{3,1},{4,6},{5,7},{6,4},{7,5},{8,10},{9,11},{10,... | collective-permute-start | bytes 393224 | tf_op jit(solution)/shard_map/ppermute | solution.py:24
  86.3 1.5 %collective-permute-start.17 = (f32[4,32,256]{2,1,0:T(8,128)S(1)}, f32[4,32,256]{2,1,0:T(8,128)S(1)}, u32[]{:S(2)}, u32[]{:S(2)}) collective-permute-start(f32[4,32,256]{2,1,0:T(8,128)S(1)} %get-tuple-element.23), channel_id=1, source_target_pairs={{0,4},{1,5},{2,6},{3,7},{4,0},{5,1},{6,2},{7,3},{8,12},{9,13},{10,... | collective-permute-start | bytes 393224 | tf_op jit(solution)/shard_map/ppermute | solution.py:24
  87.8 3.1 %collective-permute-done.19 = f32[4,32,256]{2,1,0:T(8,128)S(1)} collective-permute-done((f32[4,32,256]{2,1,0:T(8,128)S(1)}, f32[4,32,256]{2,1,0:T(8,128)S(1)}, u32[]{:S(2)}, u32[]{:S(2)}) %collective-permute-start.19) | collective-permute-done | bytes 131104 | tf_op jit(solution)/shard_map/ppermute | solution.py:24
  91.0 1.6 %collective-permute-start.20 = (f32[8,32,256]{2,1,0:T(8,128)S(1)}, f32[8,32,256]{2,1,0:T(8,128)S(1)}, u32[]{:S(2)}, u32[]{:S(2)}) collective-permute-start(f32[8,32,256]{2,1,0:T(8,128)S(1)} %bitcast.212), channel_id=1, source_target_pairs={{0,4},{1,5},{2,6},{3,7},{4,0},{5,1},{6,2},{7,3},{8,12},{9,13},{10,... | collective-permute-start | bytes 786440 | tf_op jit(solution)/shard_map/ppermute | solution.py:24
  92.7 1.7 %collective-permute-start.18 = (f32[8,32,256]{2,1,0:T(8,128)S(1)}, f32[8,32,256]{2,1,0:T(8,128)S(1)}, u32[]{:S(2)}, u32[]{:S(2)}) collective-permute-start(f32[8,32,256]{2,1,0:T(8,128)S(1)} %bitcast.214), channel_id=1, source_target_pairs={{0,2},{1,3},{2,0},{3,1},{4,6},{5,7},{6,4},{7,5},{8,10},{9,11},{10,... | collective-permute-start | bytes 786440 | tf_op jit(solution)/shard_map/ppermute | solution.py:24
  94.4 3.1 %collective-permute-done.20 = f32[8,32,256]{2,1,0:T(8,128)S(1)} collective-permute-done((f32[8,32,256]{2,1,0:T(8,128)S(1)}, f32[8,32,256]{2,1,0:T(8,128)S(1)}, u32[]{:S(2)}, u32[]{:S(2)}) %collective-permute-start.20) | collective-permute-done | bytes 262176 | tf_op jit(solution)/shard_map/ppermute | solution.py:24
  97.6 1.5 %collective-permute-done.18 = f32[8,32,256]{2,1,0:T(8,128)S(1)} collective-permute-done((f32[8,32,256]{2,1,0:T(8,128)S(1)}, f32[8,32,256]{2,1,0:T(8,128)S(1)}, u32[]{:S(2)}, u32[]{:S(2)}) %collective-permute-start.18) | collective-permute-done | bytes 262176 | tf_op jit(solution)/shard_map/ppermute | solution.py:24
  99.7 2.6 %collective-permute-done.21 = f32[16,32,512]{2,1,0:T(8,128)S(1)} collective-permute-done((f32[16,32,512]{2,1,0:T(8,128)S(1)}, f32[16,32,512]{2,1,0:T(8,128)S(1)}, u32[]{:S(2)}, u32[]{:S(2)}) %collective-permute-start.21) | collective-permute-done | bytes 1048608 | tf_op jit(solution)/shard_map/ppermute | solution.py:24
  102.3 1.0 copy-done.5
  103.3 1.7 %fusion.74 = (f32[16,1,32,512]{3,2,1,0:T(8,128)S(1)}, f32[16,1,32,512]{3,2,1,0:T(8,128)S(1)}) fusion(s32[]{:T(128)S(6)} %select_n.110, f32[1,16,32,512]{3,2,1,0:T(8,128)S(1)} %get-tuple-element.8, f32[1,16,32,512]{3,2,1,0:T(8,128)} %bitcast.211, s32[]{:T(128)S(6)} %select_n.111), kind=kLoop, calls=%fused_computation.81 | loop fusion | flops 524288 | bytes 4194312 | tf_op jit(solution)/shard_map/stack | solution.py:94
  105.2 3.8 %fusion.12 = f32[512,512]{0,1:T(8,128)S(1)} fusion(f32[1024,512]{1,0:T(8,128)S(1)} %bitcast.198, f32[4,1024,512]{2,1,0:T(8,128)} %param.4, f32[512]{0:T(512)S(1)} %bitcast.241), kind=kOutput, calls=%fused_computation.19 | convolution fusion | flops 1610874880 | bytes 5244928 | tf_op jit(solution)/shard_map/dot_general | solution.py:155
  109.1 3.5 %fusion.31 = f32[512,512]{0,1:T(8,128)S(1)} fusion(f32[512,512]{0,1:T(8,128)S(1)} %fusion.12, f32[1024,512]{1,0:T(8,128)S(1)} %bitcast.199, f32[4,1024,512]{2,1,0:T(8,128)} %param.4, f32[512]{0:T(512)S(1)} %bitcast.240), kind=kOutput, calls=%fused_computation.28 | convolution fusion | flops 1611137024 | bytes 6293504 | tf_op jit(solution)/shard_map/dot_general | solution.py:155
  112.6 1.9 %fusion.28 = f32[512,512]{0,1:T(8,128)S(1)} fusion(f32[512,512]{0,1:T(8,128)S(1)} %fusion.31, f32[1024,512]{1,0:T(8,128)S(1)} %bitcast.200, f32[4,1024,512]{2,1,0:T(8,128)S(1)} %bitcast.197, f32[512]{0:T(512)S(1)} %bitcast.239), kind=kOutput, calls=%fused_computation.27 | convolution fusion | flops 1611137024 | bytes 6293504 | tf_op jit(solution)/shard_map/dot_general | solution.py:155
  114.4 1.9 %fusion.25 = f32[512,512]{0,1:T(8,128)S(1)} fusion(f32[512,512]{0,1:T(8,128)S(1)} %fusion.28, f32[1024,512]{1,0:T(8,128)S(1)} %bitcast.201, f32[4,1024,512]{2,1,0:T(8,128)S(1)} %bitcast.197, f32[512]{0:T(512)S(1)} %bitcast.238), kind=kOutput, calls=%fused_computation.26 | convolution fusion | flops 1611137024 | bytes 6293504 | tf_op jit(solution)/shard_map/dot_general | solution.py:155
  116.6 1.8 %collective-permute-done.22 = f32[16,1,16,512]{3,2,0,1:T(8,128)S(1)} collective-permute-done((f32[16,1,16,512]{3,2,0,1:T(8,128)S(1)}, f32[16,1,16,512]{3,2,0,1:T(8,128)S(1)}, u32[]{:S(2)}, u32[]{:S(2)}) %collective-permute-start.22) | collective-permute-done | bytes 524320 | tf_op jit(solution)/shard_map/ppermute | solution.py:24
  118.5 1.7 %collective-permute-start.23 = (f32[8,1,16,256]{3,2,0,1:T(8,128)S(1)}, f32[8,1,16,256]{3,2,0,1:T(8,128)S(1)}, u32[]{:S(2)}, u32[]{:S(2)}) collective-permute-start(f32[8,1,16,256]{3,2,0,1:T(8,128)S(1)} %dynamic-slice_bitcast_fusion.3), channel_id=1, source_target_pairs={{0,2},{1,3},{2,0},{3,1},{4,6},{5,7},{6,4},{7,5},{8,10},{9,11},{10,... | collective-permute-start | bytes 393224 | tf_op jit(solution)/shard_map/ppermute | solution.py:24
  120.3 0.7 collective-permute-start.25
  121.0 3.1 %collective-permute-done.23 = f32[8,1,16,256]{3,2,0,1:T(8,128)S(1)} collective-permute-done((f32[8,1,16,256]{3,2,0,1:T(8,128)S(1)}, f32[8,1,16,256]{3,2,0,1:T(8,128)S(1)}, u32[]{:S(2)}, u32[]{:S(2)}) %collective-permute-start.23) | collective-permute-done | bytes 131104 | tf_op jit(solution)/shard_map/ppermute | solution.py:24
  124.2 0.6 collective-permute-start.24
  124.8 0.8 collective-permute-done.25
  125.6 1.0 collective-permute-start.26
  126.6 1.9 %collective-permute-done.24 = f32[4,1,16,256]{3,2,0,1:T(8,128)S(1)} collective-permute-done((f32[4,1,16,256]{3,2,0,1:T(8,128)S(1)}, f32[4,1,16,256]{3,2,0,1:T(8,128)S(1)}, u32[]{:S(2)}, u32[]{:S(2)}) %collective-permute-start.24) | collective-permute-done | bytes 65568 | tf_op jit(solution)/shard_map/ppermute | solution.py:24
  128.5 1.4 %collective-permute-done.26 = f32[4,1,16,256]{3,2,0,1:T(8,128)S(1)} collective-permute-done((f32[4,1,16,256]{3,2,0,1:T(8,128)S(1)}, f32[4,1,16,256]{3,2,0,1:T(8,128)S(1)}, u32[]{:S(2)}, u32[]{:S(2)}) %collective-permute-start.26) | collective-permute-done | bytes 65568 | tf_op jit(solution)/shard_map/ppermute | solution.py:24
  130.0 1.9 %collective-permute-start.29 = (f32[1,16,512]{2,1,0:T(8,128)S(1)}, f32[1,16,512]{2,1,0:T(8,128)S(1)}, u32[]{:S(2)}, u32[]{:S(2)}) collective-permute-start(f32[1,16,512]{2,1,0:T(8,128)S(1)} %get-tuple-element.38), channel_id=1, source_target_pairs={{0,24},{1,25},{2,26},{3,27},{4,28},{5,29},{6,30},{7,31},{8,16},{9,... | collective-permute-start | bytes 98312 | tf_op jit(solution)/shard_map/ppermute | solution.py:24
  131.9 2.6 %collective-permute-start.27 = (f32[1,16,512]{2,1,0:T(8,128)S(1)}, f32[1,16,512]{2,1,0:T(8,128)S(1)}, u32[]{:S(2)}, u32[]{:S(2)}) collective-permute-start(f32[1,16,512]{2,1,0:T(8,128)S(1)} %get-tuple-element.36), channel_id=1, source_target_pairs={{0,8},{1,9},{2,10},{3,11},{4,12},{5,13},{6,14},{7,15},{8,0},{9,1},... | collective-permute-start | bytes 98312 | tf_op jit(solution)/shard_map/ppermute | solution.py:24
  134.5 3.1 %fusion.171 = (f32[512]{0:T(512)S(1)}, f32[512,512]{0,1:T(8,128)S(1)}) fusion(f32[512,512]{0,1:T(8,128)} %get-tuple-element.47, f32[16,1,32,512]{3,2,1,0:T(8,128)S(1)} %get-tuple-element.6, f32[16,1,32,512]{3,2,1,0:T(8,128)S(1)} %get-tuple-element.5), kind=kOutput, calls=%fused_computation.248 | convolution fusion | flops 1611660800 | bytes 4196352 | tf_op jit(solution)/shard_map/dot_general | solution.py:159
  137.5 0.6 reduce_max.29
  138.9 1.4 fusion.57
  140.3 1.4 fusion.54
  142.2 1.2 fusion.48
  (92 shorter events, 9.0 us)
Async XLA Ops:
  0.6 2.7 %copy-start.1 = (f32[512,512]{1,0:T(8,128)S(1)}, f32[512,512]{1,0:T(8,128)}, u32[]{:S(2)}) copy-start(f32[512,512]{1,0:T(8,128)} %param.7) | copy-start | bytes 3145732
  0.6 2.7 %copy-start = (f32[1024,512]{1,0:T(8,128)S(1)}, f32[1024,512]{1,0:T(8,128)}, u32[]{:S(2)}) copy-start(f32[1024,512]{1,0:T(8,128)} %param.6) | copy-start | bytes 6291460
  3.4 11.6 %copy-start.2 = (f32[512,512]{0,1:T(8,128)}, f32[512,512]{0,1:T(8,128)S(1)}, u32[]{:S(2)}) copy-start(f32[512,512]{0,1:T(8,128)S(1)} %fusion.172) | copy-start | bytes 3145732
  15.0 3.2 %copy-start.8 = (f32[4,512]{1,0:T(4,128)S(1)}, f32[4,512]{1,0:T(4,128)}, u32[]{:S(2)}) copy-start(f32[4,512]{1,0:T(4,128)} %param.5) | copy-start | bytes 24580
  20.4 79.3 %copy-start.6 = (f32[4,512]{1,0:T(4,128)}, f32[4,512]{1,0:T(4,128)S(1)}, u32[]{:S(2)}) copy-start(f32[4,512]{1,0:T(4,128)S(1)} %fusion.60) | copy-start | bytes 24580
  27.9 16.8 %collective-permute-start.6 = (f32[16,1,32,512]{3,2,0,1:T(8,128)S(1)}, f32[16,1,32,512]{3,2,0,1:T(8,128)}, u32[]{:S(2)}, u32[]{:S(2)}) collective-permute-start(f32[16,1,32,512]{3,2,0,1:T(8,128)S(1)} %dynamic-slice_bitcast_fusion), channel_id=1, source_target_pairs={{0,1},{1,0},{2,3},{3,2},{4,5},{5,4},{6,7},{7,6},{8,9},{9,8},{10,11... | collective-permute-start | bytes 3145736 | tf_op jit(solution)/shard_map/ppermute | solution.py:24
  28.4 5.2 %collective-permute-start = (f32[4,512]{1,0:T(4,128)S(1)}, f32[4,512]{1,0:T(4,128)S(1)}, u32[]{:S(2)}, u32[]{:S(2)}) collective-permute-start(f32[4,512]{1,0:T(4,128)S(1)} %fusion.60), channel_id=1, source_target_pairs={{0,8},{1,9},{2,10},{3,11},{4,12},{5,13},{6,14},{7,15},{8,0},{9,1},... | collective-permute-start | bytes 24584 | tf_op jit(solution)/shard_map/ppermute | solution.py:24
  31.1 4.5 %collective-permute-start.1 = (f32[4,512]{1,0:T(4,128)S(1)}, f32[4,512]{1,0:T(4,128)S(1)}, u32[]{:S(2)}, u32[]{:S(2)}) collective-permute-start(f32[4,512]{1,0:T(4,128)S(1)} %fusion.60), channel_id=1, source_target_pairs={{0,16},{1,17},{2,18},{3,19},{4,20},{5,21},{6,22},{7,23},{8,24},{9,... | collective-permute-start | bytes 24584 | tf_op jit(solution)/shard_map/ppermute | solution.py:24
  33.7 5.4 %collective-permute-start.2 = (f32[4,512]{1,0:T(4,128)S(1)}, f32[4,512]{1,0:T(4,128)S(1)}, u32[]{:S(2)}, u32[]{:S(2)}) collective-permute-start(f32[4,512]{1,0:T(4,128)S(1)} %fusion.60), channel_id=1, source_target_pairs={{0,24},{1,25},{2,26},{3,27},{4,28},{5,29},{6,30},{7,31},{8,16},{9,... | collective-permute-start | bytes 24584 | tf_op jit(solution)/shard_map/ppermute | solution.py:24
  39.1 4.0 %collective-permute-start.3 = (f32[16,512]{1,0:T(8,128)S(1)}, f32[16,512]{1,0:T(8,128)S(1)}, u32[]{:S(2)}, u32[]{:S(2)}) collective-permute-start(f32[16,512]{1,0:T(8,128)S(1)} %pad_maximum_fusion.7), channel_id=1, source_target_pairs={{0,4},{1,5},{2,6},{3,7},{4,0},{5,1},{6,2},{7,3},{8,12},{9,13},{10,... | collective-permute-start | bytes 98312 | tf_op jit(solution)/shard_map/ppermute | solution.py:24
  43.2 4.8 %collective-permute-start.4 = (f32[32,512]{1,0:T(8,128)S(1)}, f32[32,512]{1,0:T(8,128)S(1)}, u32[]{:S(2)}, u32[]{:S(2)}) collective-permute-start(f32[32,512]{1,0:T(8,128)S(1)} %concatenate.26), channel_id=1, source_target_pairs={{0,2},{1,3},{2,0},{3,1},{4,6},{5,7},{6,4},{7,5},{8,10},{9,11},{10,... | collective-permute-start | bytes 196616 | tf_op jit(solution)/shard_map/ppermute | solution.py:24
  47.4 6.7 %collective-permute-start.7 = (f32[8,1,32,256]{3,2,0,1:T(8,128)}, f32[8,1,32,256]{3,2,0,1:T(8,128)}, u32[]{:S(2)}, u32[]{:S(2)}) collective-permute-start(f32[8,1,32,256]{3,2,0,1:T(8,128)} %dynamic-slice_bitcast_fusion.2), channel_id=1, source_target_pairs={{0,2},{1,3},{2,0},{3,1},{4,6},{5,7},{6,4},{7,5},{8,10},{9,11},{10,... | collective-permute-start | bytes 786440 | tf_op jit(solution)/shard_map/ppermute | solution.py:24
  48.0 1.5 %collective-permute-start.5 = (f32[64,512]{1,0:T(8,128)S(1)}, f32[64,512]{1,0:T(8,128)}, u32[]{:S(2)}, u32[]{:S(2)}) collective-permute-start(f32[64,512]{1,0:T(8,128)S(1)} %concatenate.27), channel_id=1, source_target_pairs={{0,1},{1,0},{2,3},{3,2},{4,5},{5,4},{6,7},{7,6},{8,9},{9,8},{10,11... | collective-permute-start | bytes 393224 | tf_op jit(solution)/shard_map/ppermute | solution.py:24
  50.5 19.5 %copy-start.3 = (f32[512,512]{0,1:T(8,128)S(1)}, f32[512,512]{0,1:T(8,128)}, u32[]{:S(2)}) copy-start(f32[512,512]{0,1:T(8,128)} %copy-done.2) | copy-start | bytes 3145732
  50.5 9.2 %collective-permute-start.9 = (f32[4,2,32,256]{3,2,0,1:T(8,128)S(1)}, f32[4,2,32,256]{3,2,0,1:T(8,128)S(1)}, u32[]{:S(2)}, u32[]{:S(2)}) collective-permute-start(f32[4,2,32,256]{3,2,0,1:T(8,128)S(1)} %bitcast.227), channel_id=1, source_target_pairs={{0,4},{1,5},{2,6},{3,7},{4,0},{5,1},{6,2},{7,3},{8,12},{9,13},{10,... | collective-permute-start | bytes 786440 | tf_op jit(solution)/shard_map/ppermute | solution.py:24
  55.1 6.7 %collective-permute-start.8 = (f32[4,1,32,256]{3,2,0,1:T(8,128)S(1)}, f32[4,1,32,256]{3,2,0,1:T(8,128)S(1)}, u32[]{:S(2)}, u32[]{:S(2)}) collective-permute-start(f32[4,1,32,256]{3,2,0,1:T(8,128)S(1)} %dynamic-slice_bitcast_fusion.4), channel_id=1, source_target_pairs={{0,4},{1,5},{2,6},{3,7},{4,0},{5,1},{6,2},{7,3},{8,12},{9,13},{10,... | collective-permute-start | bytes 393224 | tf_op jit(solution)/shard_map/ppermute | solution.py:24
  59.9 5.0 %collective-permute-start.10 = (f32[4,1,32,256]{3,2,0,1:T(8,128)S(1)}, f32[4,1,32,256]{3,2,0,1:T(8,128)S(1)}, u32[]{:S(2)}, u32[]{:S(2)}) collective-permute-start(f32[4,1,32,256]{3,2,0,1:T(8,128)S(1)} %constant_dynamic-slice_fusion.7), channel_id=1, source_target_pairs={{0,2},{1,3},{2,0},{3,1},{4,6},{5,7},{6,4},{7,5},{8,10},{9,11},{10,... | collective-permute-start | bytes 393224 | tf_op jit(solution)/shard_map/ppermute | solution.py:24
  64.9 0.8 copy-start.4
  65.6 7.3 %collective-permute-start.13 = (f32[1,32,512]{2,1,0:T(8,128)}, f32[1,32,512]{2,1,0:T(8,128)}, u32[]{:S(2)}, u32[]{:S(2)}) collective-permute-start(f32[1,32,512]{2,1,0:T(8,128)} %get-tuple-element.35), channel_id=1, source_target_pairs={{0,24},{1,25},{2,26},{3,27},{4,28},{5,29},{6,30},{7,31},{8,16},{9,... | collective-permute-start | bytes 196616 | tf_op jit(solution)/shard_map/ppermute | solution.py:24
  65.7 7.2 %collective-permute-start.12 = (f32[1,32,512]{2,1,0:T(8,128)}, f32[1,32,512]{2,1,0:T(8,128)}, u32[]{:S(2)}, u32[]{:S(2)}) collective-permute-start(f32[1,32,512]{2,1,0:T(8,128)} %get-tuple-element.34), channel_id=1, source_target_pairs={{0,16},{1,17},{2,18},{3,19},{4,20},{5,21},{6,22},{7,23},{8,24},{9,... | collective-permute-start | bytes 196616 | tf_op jit(solution)/shard_map/ppermute | solution.py:24
  65.7 7.2 %collective-permute-start.11 = (f32[1,32,512]{2,1,0:T(8,128)}, f32[1,32,512]{2,1,0:T(8,128)}, u32[]{:S(2)}, u32[]{:S(2)}) collective-permute-start(f32[1,32,512]{2,1,0:T(8,128)} %get-tuple-element.33), channel_id=1, source_target_pairs={{0,8},{1,9},{2,10},{3,11},{4,12},{5,13},{6,14},{7,15},{8,0},{9,1},... | collective-permute-start | bytes 196616 | tf_op jit(solution)/shard_map/ppermute | solution.py:24
  76.2 16.5 %copy-start.7 = (f32[32,512]{1,0:T(8,128)}, f32[32,512]{1,0:T(8,128)S(1)}, u32[]{:S(2)}) copy-start(f32[32,512]{1,0:T(8,128)S(1)} %fusion.36) | copy-start | bytes 196612
  76.2 6.1 %collective-permute-start.16 = (f32[1,32,512]{2,1,0:T(8,128)S(1)}, f32[1,32,512]{2,1,0:T(8,128)S(1)}, u32[]{:S(2)}, u32[]{:S(2)}) collective-permute-start(f32[1,32,512]{2,1,0:T(8,128)S(1)} %bitcast.228), channel_id=1, source_target_pairs={{0,24},{1,25},{2,26},{3,27},{4,28},{5,29},{6,30},{7,31},{8,16},{9,... | collective-permute-start | bytes 196616 | tf_op jit(solution)/shard_map/ppermute | solution.py:24
  78.3 5.6 %collective-permute-start.15 = (f32[1,32,512]{2,1,0:T(8,128)S(1)}, f32[1,32,512]{2,1,0:T(8,128)S(1)}, u32[]{:S(2)}, u32[]{:S(2)}) collective-permute-start(f32[1,32,512]{2,1,0:T(8,128)S(1)} %bitcast.229), channel_id=1, source_target_pairs={{0,16},{1,17},{2,18},{3,19},{4,20},{5,21},{6,22},{7,23},{8,24},{9,... | collective-permute-start | bytes 196616 | tf_op jit(solution)/shard_map/ppermute | solution.py:24
  79.4 4.9 %collective-permute-start.14 = (f32[1,32,512]{2,1,0:T(8,128)S(1)}, f32[1,32,512]{2,1,0:T(8,128)S(1)}, u32[]{:S(2)}, u32[]{:S(2)}) collective-permute-start(f32[1,32,512]{2,1,0:T(8,128)S(1)} %bitcast.230), channel_id=1, source_target_pairs={{0,8},{1,9},{2,10},{3,11},{4,12},{5,13},{6,14},{7,15},{8,0},{9,1},... | collective-permute-start | bytes 196616 | tf_op jit(solution)/shard_map/ppermute | solution.py:24
  84.5 6.4 %collective-permute-start.19 = (f32[4,32,256]{2,1,0:T(8,128)S(1)}, f32[4,32,256]{2,1,0:T(8,128)S(1)}, u32[]{:S(2)}, u32[]{:S(2)}) collective-permute-start(f32[4,32,256]{2,1,0:T(8,128)S(1)} %get-tuple-element.26), channel_id=1, source_target_pairs={{0,2},{1,3},{2,0},{3,1},{4,6},{5,7},{6,4},{7,5},{8,10},{9,11},{10,... | collective-permute-start | bytes 393224 | tf_op jit(solution)/shard_map/ppermute | solution.py:24
  86.3 6.3 %collective-permute-start.17 = (f32[4,32,256]{2,1,0:T(8,128)S(1)}, f32[4,32,256]{2,1,0:T(8,128)S(1)}, u32[]{:S(2)}, u32[]{:S(2)}) collective-permute-start(f32[4,32,256]{2,1,0:T(8,128)S(1)} %get-tuple-element.23), channel_id=1, source_target_pairs={{0,4},{1,5},{2,6},{3,7},{4,0},{5,1},{6,2},{7,3},{8,12},{9,13},{10,... | collective-permute-start | bytes 393224 | tf_op jit(solution)/shard_map/ppermute | solution.py:24
  91.0 6.4 %collective-permute-start.20 = (f32[8,32,256]{2,1,0:T(8,128)S(1)}, f32[8,32,256]{2,1,0:T(8,128)S(1)}, u32[]{:S(2)}, u32[]{:S(2)}) collective-permute-start(f32[8,32,256]{2,1,0:T(8,128)S(1)} %bitcast.212), channel_id=1, source_target_pairs={{0,4},{1,5},{2,6},{3,7},{4,0},{5,1},{6,2},{7,3},{8,12},{9,13},{10,... | collective-permute-start | bytes 786440 | tf_op jit(solution)/shard_map/ppermute | solution.py:24
  92.7 6.4 %collective-permute-start.18 = (f32[8,32,256]{2,1,0:T(8,128)S(1)}, f32[8,32,256]{2,1,0:T(8,128)S(1)}, u32[]{:S(2)}, u32[]{:S(2)}) collective-permute-start(f32[8,32,256]{2,1,0:T(8,128)S(1)} %bitcast.214), channel_id=1, source_target_pairs={{0,2},{1,3},{2,0},{3,1},{4,6},{5,7},{6,4},{7,5},{8,10},{9,11},{10,... | collective-permute-start | bytes 786440 | tf_op jit(solution)/shard_map/ppermute | solution.py:24
  99.6 2.7 %collective-permute-start.21 = (f32[16,32,512]{2,1,0:T(8,128)S(1)}, f32[16,32,512]{2,1,0:T(8,128)S(1)}, u32[]{:S(2)}, u32[]{:S(2)}) collective-permute-start(f32[16,32,512]{2,1,0:T(8,128)S(1)} %get-tuple-element.7), channel_id=1, source_target_pairs={{0,1},{1,0},{2,3},{3,2},{4,5},{5,4},{6,7},{7,6},{8,9},{9,8},{10,11... | collective-permute-start | bytes 3145736 | tf_op jit(solution)/shard_map/ppermute | solution.py:24
  102.3 1.0 copy-start.5
  105.0 7.5 %slice-start = ((s8[8388608]{0:T(1024)(128)(4,1)}), s8[4194304]{0:T(1024)(128)(4,1)S(1)}, s32[]{:S(2)}) async-start(s8[8388608]{0:T(1024)(128)(4,1)} %bitcast.196), calls=%async_computation | async-start | bytes 8388608
  105.2 7.3 %slice-start.1 = ((s8[8388608]{0:T(1024)(128)(4,1)}), s8[4194304]{0:T(1024)(128)(4,1)S(1)}, s32[]{:S(2)}) async-start(s8[8388608]{0:T(1024)(128)(4,1)} %bitcast.196), calls=%async_computation.1 | async-start | bytes 8388608
  116.4 2.0 %collective-permute-start.22 = (f32[16,1,16,512]{3,2,0,1:T(8,128)S(1)}, f32[16,1,16,512]{3,2,0,1:T(8,128)S(1)}, u32[]{:S(2)}, u32[]{:S(2)}) collective-permute-start(f32[16,1,16,512]{3,2,0,1:T(8,128)S(1)} %dynamic-slice_bitcast_fusion.1), channel_id=1, source_target_pairs={{0,1},{1,0},{2,3},{3,2},{4,5},{5,4},{6,7},{7,6},{8,9},{9,8},{10,11... | collective-permute-start | bytes 1572872 | tf_op jit(solution)/shard_map/ppermute | solution.py:24
  118.5 5.6 %collective-permute-start.23 = (f32[8,1,16,256]{3,2,0,1:T(8,128)S(1)}, f32[8,1,16,256]{3,2,0,1:T(8,128)S(1)}, u32[]{:S(2)}, u32[]{:S(2)}) collective-permute-start(f32[8,1,16,256]{3,2,0,1:T(8,128)S(1)} %dynamic-slice_bitcast_fusion.3), channel_id=1, source_target_pairs={{0,2},{1,3},{2,0},{3,1},{4,6},{5,7},{6,4},{7,5},{8,10},{9,11},{10,... | collective-permute-start | bytes 393224 | tf_op jit(solution)/shard_map/ppermute | solution.py:24
  120.3 5.3 %collective-permute-start.25 = (f32[4,2,16,256]{3,2,0,1:T(8,128)S(1)}, f32[4,2,16,256]{3,2,0,1:T(8,128)S(1)}, u32[]{:S(2)}, u32[]{:S(2)}) collective-permute-start(f32[4,2,16,256]{3,2,0,1:T(8,128)S(1)} %bitcast.232), channel_id=1, source_target_pairs={{0,4},{1,5},{2,6},{3,7},{4,0},{5,1},{6,2},{7,3},{8,12},{9,13},{10,... | collective-permute-start | bytes 393224 | tf_op jit(solution)/shard_map/ppermute | solution.py:24
  124.2 4.3 %collective-permute-start.24 = (f32[4,1,16,256]{3,2,0,1:T(8,128)S(1)}, f32[4,1,16,256]{3,2,0,1:T(8,128)S(1)}, u32[]{:S(2)}, u32[]{:S(2)}) collective-permute-start(f32[4,1,16,256]{3,2,0,1:T(8,128)S(1)} %dynamic-slice_bitcast_fusion.5), channel_id=1, source_target_pairs={{0,4},{1,5},{2,6},{3,7},{4,0},{5,1},{6,2},{7,3},{8,12},{9,13},{10,... | collective-permute-start | bytes 196616 | tf_op jit(solution)/shard_map/ppermute | solution.py:24
  125.6 4.3 %collective-permute-start.26 = (f32[4,1,16,256]{3,2,0,1:T(8,128)S(1)}, f32[4,1,16,256]{3,2,0,1:T(8,128)S(1)}, u32[]{:S(2)}, u32[]{:S(2)}) collective-permute-start(f32[4,1,16,256]{3,2,0,1:T(8,128)S(1)} %constant_dynamic-slice_fusion), channel_id=1, source_target_pairs={{0,2},{1,3},{2,0},{3,1},{4,6},{5,7},{6,4},{7,5},{8,10},{9,11},{10,... | collective-permute-start | bytes 196616 | tf_op jit(solution)/shard_map/ppermute | solution.py:24
  130.0 8.8 %collective-permute-start.29 = (f32[1,16,512]{2,1,0:T(8,128)S(1)}, f32[1,16,512]{2,1,0:T(8,128)S(1)}, u32[]{:S(2)}, u32[]{:S(2)}) collective-permute-start(f32[1,16,512]{2,1,0:T(8,128)S(1)} %get-tuple-element.38), channel_id=1, source_target_pairs={{0,24},{1,25},{2,26},{3,27},{4,28},{5,29},{6,30},{7,31},{8,16},{9,... | collective-permute-start | bytes 98312 | tf_op jit(solution)/shard_map/ppermute | solution.py:24
  131.9 7.0 %collective-permute-start.28 = (f32[1,16,512]{2,1,0:T(8,128)S(1)}, f32[1,16,512]{2,1,0:T(8,128)S(1)}, u32[]{:S(2)}, u32[]{:S(2)}) collective-permute-start(f32[1,16,512]{2,1,0:T(8,128)S(1)} %get-tuple-element.37), channel_id=1, source_target_pairs={{0,16},{1,17},{2,18},{3,19},{4,20},{5,21},{6,22},{7,23},{8,24},{9,... | collective-permute-start | bytes 98312 | tf_op jit(solution)/shard_map/ppermute | solution.py:24
  131.9 7.0 %collective-permute-start.27 = (f32[1,16,512]{2,1,0:T(8,128)S(1)}, f32[1,16,512]{2,1,0:T(8,128)S(1)}, u32[]{:S(2)}, u32[]{:S(2)}) collective-permute-start(f32[1,16,512]{2,1,0:T(8,128)S(1)} %get-tuple-element.36), channel_id=1, source_target_pairs={{0,8},{1,9},{2,10},{3,11},{4,12},{5,13},{6,14},{7,15},{8,0},{9,1},... | collective-permute-start | bytes 98312 | tf_op jit(solution)/shard_map/ppermute | solution.py:24
